TPU v7x, 32 devices: a whole 2x2x4 slice. The times are simulated.
32 devices in a mesh: dp: 2 (over x), row: 4 (over z), col: 4 (over y, core).
Axes of the slice: x: 2, y: 2, z: 4, core: 2. Of those that a mesh axis runs over, the one named last changes fastest.
Arguments:
- tokens: bfloat16 [4, 2048, 2048], P('dp', 'row', 'col'), may hold values from -6 to 6
- lengths: int32 [4], P('dp'), may hold values from 682 to 2048, as said below
- cotangent: bfloat16 [4, 2048, 2048], P('dp', 'row', 'col'), may hold values from -6 to 6
- norm1_gain: float32 [2048], P('col'), may hold values from 0.25 to 1.75
- norm1_bias: float32 [2048], P('col'), may hold values from -3 to 3
- query_weight: bfloat16 [2048, 2048], P('col', 'row'), may hold values from -0.125 to 0.125
- kv_weight: bfloat16 [2048, 256], P('col'), may hold values from -0.125 to 0.125
- out_weight: bfloat16 [2048, 2048], P('row', 'col'), may hold values from -1 to 1
- norm2_gain: float32 [2048], P('col'), may hold values from 0.25 to 1.75
- norm2_bias: float32 [2048], P('col'), may hold values from -3 to 3
- up_weight: bfloat16 [2048, 8192], P('col', 'row'), may hold values from -0.125 to 0.125
- down_weight: bfloat16 [8192, 2048], P('row', 'col'), may hold values from -0.0625 to 0.0625
Outputs:
- out: bfloat16 [4, 2048, 2048], P('dp', 'row', 'col')
- grad_input: bfloat16 [4, 2048, 2048], P('dp', 'row', 'col')
- grad_norm1_gain: float32 [2048], P('col')
- grad_norm1_bias: float32 [2048], P('col')
- grad_query_weight: float32 [2048, 2048], P('col', 'row')
- grad_kv_weight: float32 [2048, 256], P('col')
- grad_out_weight: float32 [2048, 2048], P('row', 'col')
- grad_norm2_gain: float32 [2048], P('col')
- grad_norm2_bias: float32 [2048], P('col')
- grad_up_weight: float32 [2048, 8192], P('col', 'row')
- grad_down_weight: float32 [8192, 2048], P('row', 'col')
Inputs may be any that keep to these rules, and one draw needn't show every extreme that they name: `lengths`: entry s is the number of valid slots of sequence s; sequences s * 2 to s * 2 + 1 belong to index s of dp. Some sequence has all 2048 slots valid.
All inputs are finite; a program needn't handle non-finite values.
Results may differ from a plain program's by a relative error of at most 0.02.
Values may be sent and summed in bfloat16 or wider, within the bound.
A program may use at most 256 MiB of HBM per device.

v0:
```python
from functools import partial

import jax
import jax.numpy as jnp
from jax import lax
from jax.sharding import PartitionSpec as P

eps = 1e-05


def as_sent(x):

    def short(part):
        return part.astype(jnp.bfloat16) if part.dtype == jnp.float32 else part

    return jax.tree.map(short, x)


def contract_rows(left_side, right_side):
    return lax.dot_general(
        left_side, right_side, (((0,), (0,)), ((), ())), preferred_element_type=jnp.float32
    )


def contract_cols(left_side, right_side):
    return lax.dot_general(
        left_side, right_side, (((1,), (1,)), ((), ())), preferred_element_type=jnp.float32
    )


def slice_product(left_side, right_side, first_row, count_rows, flipped):
    picked = lax.dynamic_slice_in_dim(left_side, first_row, count_rows, 0)
    if flipped:
        return contract_cols(picked, right_side)
    return jnp.dot(picked, right_side, preferred_element_type=jnp.float32)


def feature_moments(first_terms, second_terms):
    return lax.psum((first_terms, second_terms), "col")


def norm_forward(hidden, norm_gain, norm_bias, row_keep):
    feature_count = hidden.shape[1] * lax.axis_size("col")
    totals, squares = feature_moments(jnp.sum(hidden, axis=1), jnp.sum(hidden * hidden, axis=1))
    centre = totals / feature_count
    spread = squares / feature_count - centre * centre
    inverse = lax.rsqrt(spread + eps)
    normed = (hidden - centre[:, None]) * inverse[:, None]
    return (normed, inverse, (row_keep * (normed * norm_gain + norm_bias)).astype(jnp.bfloat16))


def norm_backward(gradient, normed, inverse, norm_gain, row_keep):
    feature_count = gradient.shape[1] * lax.axis_size("col")
    masked = row_keep * gradient
    scaled = masked * norm_gain
    first_mean, second_mean = feature_moments(
        jnp.sum(scaled, axis=1), jnp.sum(scaled * normed, axis=1)
    )
    result = inverse[:, None] * (
        scaled
        - first_mean[:, None] / feature_count
        - normed * (second_mean[:, None] / feature_count)
    )
    return (result, jnp.sum(masked * normed, axis=0), jnp.sum(masked, axis=0))


def gather_rows(hidden):
    return lax.all_gather(hidden, "row", axis=0, tiled=True)


def gather_cols(hidden):
    return jax.tree.map(
        lambda part, own: part.astype(own.dtype),
        lax.all_gather(as_sent(hidden), "col", axis=0, tiled=True),
        hidden,
    )


def gather_grad_rows(hidden):
    return lax.all_gather(hidden, "row", axis=0, tiled=True)


def gather_grad_cols(hidden):
    return lax.all_gather(hidden, "col", axis=0, tiled=True)


def reduce_cols(left_side, right_side):

    def partial_term(first_row, count_rows):
        return slice_product(left_side, right_side, first_row, count_rows, False)

    return lax.psum_scatter(
        partial_term(
            jnp.int32(0), lax.axis_size("col") * (left_side.shape[0] // lax.axis_size("col"))
        ),
        "col",
        scatter_dimension=0,
        tiled=True,
    )


def reduce_rows(left_side, right_side):

    def partial_term(first_row, count_rows):
        return slice_product(left_side, right_side, first_row, count_rows, False)

    return lax.psum_scatter(
        partial_term(
            jnp.int32(0), left_side.shape[0] // lax.axis_size("row") * lax.axis_size("row")
        ).astype(jnp.bfloat16),
        "row",
        scatter_dimension=0,
        tiled=True,
    ).astype(jnp.float32)


def reduce_grad_cols(left_side, right_side):

    def partial_term(first_row, count_rows):
        return slice_product(left_side, right_side, first_row, count_rows, True)

    return lax.psum_scatter(
        partial_term(
            jnp.int32(0), left_side.shape[0] // lax.axis_size("col") * lax.axis_size("col")
        ).astype(jnp.bfloat16),
        "col",
        scatter_dimension=0,
        tiled=True,
    ).astype(jnp.float32)


def reduce_grad_rows(left_side, right_side):

    def partial_term(first_row, count_rows):
        return slice_product(left_side, right_side, first_row, count_rows, True)

    return lax.psum_scatter(
        partial_term(
            jnp.int32(0), left_side.shape[0] // lax.axis_size("row") * lax.axis_size("row")
        ).astype(jnp.bfloat16),
        "row",
        scatter_dimension=0,
        tiled=True,
    ).astype(jnp.float32)


def valid_pairs(query_first, query_count, key_count, seq_length):
    query_pos = query_first + jnp.arange(query_count, dtype=jnp.int32)[:, None]
    key_pos = jnp.arange(key_count, dtype=jnp.int32)[None, :]
    return (key_pos <= query_pos) & (key_pos < seq_length)


def head_scores(query_head, key_rows, allowed):
    scaling = query_head.shape[1] ** (-0.5)
    scores = contract_cols(query_head, key_rows) * scaling
    return jnp.where(allowed, scores, -jnp.inf)


def attend_forward(queries, key_rows, value_rows, allowed):
    head_size = key_rows.shape[1]
    head_count = queries.shape[1] // head_size

    def one_head(head_index, loop_state):
        outputs, log_totals = loop_state
        query_head = lax.dynamic_slice_in_dim(queries, head_index * head_size, head_size, 1)
        scores = head_scores(query_head, key_rows, allowed)
        row_max = jnp.max(scores, axis=1, keepdims=True)
        log_total = row_max + jnp.log(jnp.sum(jnp.exp(scores - row_max), axis=1, keepdims=True))
        weights = jnp.exp(scores - log_total).astype(jnp.bfloat16)
        result = jnp.dot(weights, value_rows, preferred_element_type=jnp.float32).astype(
            jnp.bfloat16
        )
        outputs = lax.dynamic_update_slice_in_dim(outputs, result, head_index * head_size, 1)
        log_totals = lax.dynamic_update_slice_in_dim(log_totals, log_total, head_index, 1)
        return (outputs, log_totals)

    start_out = jnp.zeros(queries.shape, jnp.bfloat16)
    start_log = jnp.zeros((queries.shape[0], head_count), jnp.float32)
    return lax.fori_loop(0, head_count, one_head, (start_out, start_log))


def attend_backward(queries, key_rows, value_rows, allowed, log_totals, grad_out):
    head_size = key_rows.shape[1]
    head_count = queries.shape[1] // head_size
    scaling = head_size ** (-0.5)

    def one_head(head_index, loop_state):
        grad_queries, grad_keys, grad_values = loop_state
        query_head = lax.dynamic_slice_in_dim(queries, head_index * head_size, head_size, 1)
        grad_head = lax.dynamic_slice_in_dim(grad_out, head_index * head_size, head_size, 1)
        scores = head_scores(query_head, key_rows, allowed)
        weights = jnp.exp(scores - lax.dynamic_slice_in_dim(log_totals, head_index, 1, 1))
        grad_weights = contract_cols(grad_head, value_rows)
        grad_scores = (
            weights * (grad_weights - jnp.sum(weights * grad_weights, axis=1, keepdims=True))
        ).astype(jnp.bfloat16)
        grad_query = jnp.dot(grad_scores, key_rows, preferred_element_type=jnp.float32) * scaling
        grad_queries = lax.dynamic_update_slice_in_dim(
            grad_queries, grad_query, head_index * head_size, 1
        )
        grad_keys = grad_keys + contract_rows(grad_scores, query_head) * scaling
        grad_values = grad_values + contract_rows(weights.astype(jnp.bfloat16), grad_head)
        return (grad_queries, grad_keys, grad_values)

    start_queries = jnp.zeros(queries.shape, jnp.float32)
    start_keys = jnp.zeros(key_rows.shape, jnp.float32)
    start_values = jnp.zeros(value_rows.shape, jnp.float32)
    return lax.fori_loop(0, head_count, one_head, (start_queries, start_keys, start_values))


def local(
    tokens,
    lengths,
    cotangent,
    norm1_gain,
    norm1_bias,
    query_weight,
    kv_weight,
    out_weight,
    norm2_gain,
    norm2_bias,
    up_weight,
    down_weight,
):
    local_rows = tokens.shape[1]
    row_first = lax.axis_index("row") * local_rows
    slot_count = local_rows * lax.axis_size("row")
    query_rows = slot_count // lax.axis_size("col")
    query_first = lax.axis_index("col") * query_rows
    head_size = kv_weight.shape[1] // 2
    query_total = jnp.zeros(query_weight.shape, jnp.float32)
    kv_total = jnp.zeros(kv_weight.shape, jnp.float32)
    out_total = jnp.zeros(out_weight.shape, jnp.float32)
    up_total = jnp.zeros(up_weight.shape, jnp.float32)
    down_total = jnp.zeros(down_weight.shape, jnp.float32)
    gain_one_total = jnp.zeros(norm1_gain.shape, jnp.float32)
    bias_one_total = jnp.zeros(norm1_gain.shape, jnp.float32)
    gain_two_total = jnp.zeros(norm1_gain.shape, jnp.float32)
    bias_two_total = jnp.zeros(norm1_gain.shape, jnp.float32)
    outputs_list = []
    grads_list = []
    for micro_index in range(tokens.shape[0]):
        seq_length = lengths[micro_index]
        row_keep = (row_first + jnp.arange(local_rows, dtype=jnp.int32) < seq_length).astype(
            jnp.float32
        )[:, None]
        allowed = valid_pairs(query_first, query_rows, slot_count, seq_length)
        hidden = tokens[micro_index].astype(jnp.float32)
        normed_one, inverse_one, input_one = norm_forward(hidden, norm1_gain, norm1_bias, row_keep)
        gathered_one = gather_rows(input_one)
        queries = reduce_cols(gathered_one, query_weight).astype(jnp.bfloat16)
        key_value = lax.psum(
            jnp.dot(gathered_one, kv_weight, preferred_element_type=jnp.float32), "col"
        ).astype(jnp.bfloat16)
        key_rows = key_value[:, :head_size]
        value_rows = key_value[:, head_size:]
        attended, log_totals = attend_forward(queries, key_rows, value_rows, allowed)
        attended_all = gather_cols(attended)
        middle = hidden + reduce_rows(attended_all, out_weight)
        normed_two, inverse_two, input_two = norm_forward(middle, norm2_gain, norm2_bias, row_keep)
        gathered_two = gather_rows(input_two)
        up_sums = reduce_cols(gathered_two, up_weight)
        activated, gelu_pull = jax.vjp(partial(jax.nn.gelu, approximate=True), up_sums)
        activated_all = gather_cols(activated.astype(jnp.bfloat16))
        final_out = row_keep * (middle + reduce_rows(activated_all, down_weight))
        outputs_list.append(final_out.astype(jnp.bfloat16))
        grad_final = row_keep * cotangent[micro_index].astype(jnp.float32)
        grad_ffn_all = gather_grad_rows(grad_final.astype(jnp.bfloat16))
        grad_down = contract_rows(activated_all, grad_ffn_all)
        grad_activated = reduce_grad_cols(grad_ffn_all, down_weight)
        grad_up_sums = gelu_pull(grad_activated)[0]
        grad_up_all = gather_grad_cols(grad_up_sums.astype(jnp.bfloat16))
        grad_up = contract_rows(gathered_two, grad_up_all)
        up_total = up_total + grad_up
        down_total = down_total + grad_down
        grad_input_two = reduce_grad_rows(grad_up_all, up_weight)
        grad_norm_two, gain_two, bias_two = norm_backward(
            grad_input_two, normed_two, inverse_two, norm2_gain, row_keep
        )
        grad_middle = grad_final + grad_norm_two
        grad_attn_all = gather_grad_rows(grad_middle.astype(jnp.bfloat16))
        grad_out = contract_rows(attended_all, grad_attn_all)
        grad_attended = reduce_grad_cols(grad_attn_all, out_weight).astype(jnp.bfloat16)
        grad_queries, grad_keys, grad_values = attend_backward(
            queries, key_rows, value_rows, allowed, log_totals, grad_attended
        )
        grad_key_value = lax.psum(
            jnp.concatenate([grad_keys, grad_values], axis=1).astype(jnp.bfloat16), ("row", "col")
        )
        grad_query_all = gather_grad_cols(grad_queries.astype(jnp.bfloat16))
        grad_query = contract_rows(gathered_one, grad_query_all)
        grad_kv = contract_rows(gathered_one, grad_key_value)
        grad_input_one = reduce_grad_rows(grad_query_all, query_weight) + slice_product(
            grad_key_value, kv_weight, row_first, local_rows, True
        )
        grad_norm_one, gain_one, bias_one = norm_backward(
            grad_input_one, normed_one, inverse_one, norm1_gain, row_keep
        )
        grads_list.append((grad_middle + grad_norm_one).astype(jnp.bfloat16))
        query_total = query_total + grad_query
        kv_total = kv_total + grad_kv
        out_total = out_total + grad_out
        gain_one_total = gain_one_total + gain_one
        bias_one_total = bias_one_total + bias_one
        gain_two_total = gain_two_total + gain_two
        bias_two_total = bias_two_total + bias_two
    query_total, kv_total, out_total, up_total, down_total = (
        lax.psum(query_total.astype(jnp.bfloat16), "dp").astype(jnp.float32),
        lax.psum(kv_total.astype(jnp.bfloat16), "dp").astype(jnp.float32),
        lax.psum(out_total.astype(jnp.bfloat16), "dp").astype(jnp.float32),
        lax.psum(up_total.astype(jnp.bfloat16), "dp").astype(jnp.float32),
        lax.psum(down_total.astype(jnp.bfloat16), "dp").astype(jnp.float32),
    )
    gain_one_total, bias_one_total, gain_two_total, bias_two_total = lax.psum(
        (gain_one_total, bias_one_total, gain_two_total, bias_two_total), ("dp", "row")
    )
    return (
        jnp.stack(outputs_list),
        jnp.stack(grads_list),
        gain_one_total,
        bias_one_total,
        query_total,
        kv_total,
        out_total,
        gain_two_total,
        bias_two_total,
        up_total,
        down_total,
    )


def solution(mesh):
    placed = (
        P("dp", "row", "col"),
        P("dp"),
        P("dp", "row", "col"),
        P("col"),
        P("col"),
        P("col", "row"),
        P("col", None),
        P("row", "col"),
        P("col"),
        P("col"),
        P("col", "row"),
        P("row", "col"),
    )
    return jax.shard_map(
        local,
        mesh=mesh,
        in_specs=placed,
        out_specs=(
            P("dp", "row", "col"),
            P("dp", "row", "col"),
            P("col"),
            P("col"),
            P("col", "row"),
            P("col", None),
            P("row", "col"),
            P("col"),
            P("col"),
            P("col", "row"),
            P("row", "col"),
        ),
        check_vma=False,
    )
```

profile of v0, /device:TPU:0, one launch (start us, length us, event | category | flops | bytes accessed | tf_op | source)
XLA Modules:
  0.0 2029.3 jit_solution(2918229098984352749)
XLA Ops:
  13.0 8.5 all-reduce.5
  25.2 45.6 %all-gather.17.cloned.1.call-done = bf16[2048,512]{1,0:T(8,128)(2,1)} async-done(((bf16[512,512]{1,0:T(8,128)(2,1)}), bf16[2048,512]{1,0:T(8,128)(2,1)}) %all-gather.17.cloned.1.call-update) | async-done | bytes 2097168 | tf_op jit(solution)/shard_map/all_gather | solution.py:68
  77.1 40.5 %all-gather.25.cloned.1.call-done = bf16[2048,512]{1,0:T(8,128)(2,1)} async-done(((bf16[512,512]{1,0:T(8,128)(2,1)}), bf16[2048,512]{1,0:T(8,128)(2,1)}) %all-gather.25.cloned.1.call-update) | async-done | bytes 2097168 | tf_op jit(solution)/shard_map/all_gather | solution.py:68
  129.6 116.3 %all-reduce.15 = (bf16[2048,256]{1,0:T(8,128)(2,1)}, bf16[2048,256]{1,0:T(8,128)(2,1)}) all-reduce(f32[2048,256]{1,0:T(8,128)} %fusion.143, f32[2048,256]{1,0:T(8,128)} %fusion.146), channel_id=1, replica_groups=mesh['dp'=2,'row'=4,'col'=4] {'col'}, use_global_device_ids=true, to_apply=%region_5.0 | all-reduce | flops 1048576 | bytes 6291456 | tf_op jit(solution)/shard_map/psum | solution.py:252
  253.1 18.9 while.68
  275.1 18.9 while.69
  298.7 19.5 all-gather.27.cloned.1.call-done
  322.5 42.4 %reduce-scatter.19.cloned.1.call-done = bf16[512,512]{1,0:T(8,128)(2,1)} async-done(((bf16[2048,512]{1,0:T(8,128)(2,1)}), bf16[512,512]{1,0:T(8,128)(2,1)}) %reduce-scatter.19.cloned.1.call-update) | async-done | bytes 524304 | tf_op jit(solution)/shard_map/reduce_scatter | solution.py:107
  365.0 46.2 %reduce-scatter.27.cloned.1.call-done = bf16[512,512]{1,0:T(8,128)(2,1)} async-done(((bf16[2048,512]{1,0:T(8,128)(2,1)}), bf16[512,512]{1,0:T(8,128)(2,1)}) %reduce-scatter.27.cloned.1.call-update) | async-done | bytes 524304 | tf_op jit(solution)/shard_map/reduce_scatter | solution.py:107
  412.9 6.5 all-reduce.3
  424.6 43.0 %all-gather.33.cloned.1.call-done = bf16[2048,512]{1,0:T(8,128)(2,1)} async-done(((bf16[512,512]{1,0:T(8,128)(2,1)}), bf16[2048,512]{1,0:T(8,128)(2,1)}) %all-gather.33.cloned.1.call-update) | async-done | bytes 2097168 | tf_op jit(solution)/shard_map/all_gather | solution.py:80
  467.6 10.0 convolution_convert_fusion.1
  477.7 36.6 %all-gather.21.cloned.1.call-done = bf16[2048,512]{1,0:T(8,128)(2,1)} async-done(((bf16[512,512]{1,0:T(8,128)(2,1)}), bf16[2048,512]{1,0:T(8,128)(2,1)}) %all-gather.21.cloned.1.call-update) | async-done | bytes 2097168 | tf_op jit(solution)/shard_map/all_gather | solution.py:68
  514.3 10.0 fusion.144
  524.8 36.3 %all-gather.41.cloned.1.call-done = bf16[2048,512]{1,0:T(8,128)(2,1)} async-done(((bf16[512,512]{1,0:T(8,128)(2,1)}), bf16[2048,512]{1,0:T(8,128)(2,1)}) %all-gather.41.cloned.1.call-update) | async-done | bytes 2097168 | tf_op jit(solution)/shard_map/all_gather | solution.py:80
  561.1 10.0 convolution_convert_fusion
  571.2 36.6 %all-gather.29.cloned.1.call-done = bf16[2048,512]{1,0:T(8,128)(2,1)} async-done(((bf16[512,512]{1,0:T(8,128)(2,1)}), bf16[2048,512]{1,0:T(8,128)(2,1)}) %all-gather.29.cloned.1.call-update) | async-done | bytes 2097168 | tf_op jit(solution)/shard_map/all_gather | solution.py:68
  607.8 11.4 fusion.147
  619.3 61.5 %reduce-scatter.33.cloned.1.call-done = bf16[512,2048]{1,0:T(8,128)(2,1)} async-done(((bf16[2048,2048]{1,0:T(8,128)(2,1)}), bf16[512,2048]{1,0:T(8,128)(2,1)}) %reduce-scatter.33.cloned.1.call-update) | async-done | bytes 2097168 | tf_op jit(solution)/shard_map/reduce_scatter | solution.py:122
  680.8 128.8 %reduce-scatter.21.cloned.1.call-done = f32[512,2048]{1,0:T(8,128)} async-done(((f32[2048,2048]{1,0:T(8,128)}), f32[512,2048]{1,0:T(8,128)}) %reduce-scatter.21.cloned.1.call-update) | async-done | bytes 4194320 | tf_op jit(solution)/shard_map/reduce_scatter | solution.py:92
  816.7 67.1 %reduce-scatter.41.cloned.1.call-done = bf16[512,2048]{1,0:T(8,128)(2,1)} async-done(((bf16[2048,2048]{1,0:T(8,128)(2,1)}), bf16[512,2048]{1,0:T(8,128)(2,1)}) %reduce-scatter.41.cloned.1.call-update) | async-done | bytes 2097168 | tf_op jit(solution)/shard_map/reduce_scatter | solution.py:122
  883.8 128.8 %reduce-scatter.29.cloned.1.call-done = f32[512,2048]{1,0:T(8,128)} async-done(((f32[2048,2048]{1,0:T(8,128)}), f32[512,2048]{1,0:T(8,128)}) %reduce-scatter.29.cloned.1.call-update) | async-done | bytes 4194320 | tf_op jit(solution)/shard_map/reduce_scatter | solution.py:92
  1019.9 53.0 %all-gather.23.cloned.1.call-done = bf16[2048,2048]{1,0:T(8,128)(2,1)} async-done(((bf16[512,2048]{1,0:T(8,128)(2,1)}), bf16[2048,2048]{1,0:T(8,128)(2,1)}) %all-gather.23.cloned.1.call-update) | async-done | bytes 8388624 | tf_op jit(solution)/shard_map/all_gather | solution.py:74
  1072.9 9.8 convolution_convert_fusion.10
  1082.8 50.4 %all-gather.35.cloned.1.call-done = bf16[2048,2048]{1,0:T(8,128)(2,1)} async-done(((bf16[512,2048]{1,0:T(8,128)(2,1)}), bf16[2048,2048]{1,0:T(8,128)(2,1)}) %all-gather.35.cloned.1.call-update) | async-done | bytes 8388624 | tf_op jit(solution)/shard_map/all_gather | solution.py:84
  1133.2 9.1 convolution_convert_fusion.7
  1142.4 50.7 %all-gather.43.cloned.1.call-done = bf16[2048,2048]{1,0:T(8,128)(2,1)} async-done(((bf16[512,2048]{1,0:T(8,128)(2,1)}), bf16[2048,2048]{1,0:T(8,128)(2,1)}) %all-gather.43.cloned.1.call-update) | async-done | bytes 8388624 | tf_op jit(solution)/shard_map/all_gather | solution.py:84
  1193.1 9.1 convolution_convert_fusion.4
  1202.5 50.3 %all-gather.31.cloned.1.call-done = bf16[2048,2048]{1,0:T(8,128)(2,1)} async-done(((bf16[512,2048]{1,0:T(8,128)(2,1)}), bf16[2048,2048]{1,0:T(8,128)(2,1)}) %all-gather.31.cloned.1.call-update) | async-done | bytes 8388624 | tf_op jit(solution)/shard_map/all_gather | solution.py:74
  1252.8 9.8 convolution_convert_fusion.8
  1262.7 36.3 %reduce-scatter.23.cloned.1.call-done = bf16[512,512]{1,0:T(8,128)(2,1)} async-done(((bf16[2048,512]{1,0:T(8,128)(2,1)}), bf16[512,512]{1,0:T(8,128)(2,1)}) %reduce-scatter.23.cloned.1.call-update) | async-done | bytes 524304 | tf_op jit(solution)/shard_map/reduce_scatter | solution.py:107
  1299.0 46.2 %reduce-scatter.35.cloned.1.call-done = bf16[512,512]{1,0:T(8,128)(2,1)} async-done(((bf16[2048,512]{1,0:T(8,128)(2,1)}), bf16[512,512]{1,0:T(8,128)(2,1)}) %reduce-scatter.35.cloned.1.call-update) | async-done | bytes 524304 | tf_op jit(solution)/shard_map/reduce_scatter | solution.py:137
  1345.2 46.1 %reduce-scatter.43.cloned.1.call-done = bf16[512,512]{1,0:T(8,128)(2,1)} async-done(((bf16[2048,512]{1,0:T(8,128)(2,1)}), bf16[512,512]{1,0:T(8,128)(2,1)}) %reduce-scatter.43.cloned.1.call-update) | async-done | bytes 524304 | tf_op jit(solution)/shard_map/reduce_scatter | solution.py:137
  1391.3 45.5 %reduce-scatter.31.cloned.1.call-done = bf16[512,512]{1,0:T(8,128)(2,1)} async-done(((bf16[2048,512]{1,0:T(8,128)(2,1)}), bf16[512,512]{1,0:T(8,128)(2,1)}) %reduce-scatter.31.cloned.1.call-update) | async-done | bytes 524304 | tf_op jit(solution)/shard_map/reduce_scatter | solution.py:107
  1440.9 6.5 all-reduce.2
  1451.5 44.4 %all-gather.45.cloned.1.call-done = bf16[2048,512]{1,0:T(8,128)(2,1)} async-done(((bf16[512,512]{1,0:T(8,128)(2,1)}), bf16[2048,512]{1,0:T(8,128)(2,1)}) %all-gather.45.cloned.1.call-update) | async-done | bytes 2097168 | tf_op jit(solution)/shard_map/all_gather | solution.py:80
  1500.3 42.3 %all-gather.37.cloned.1.call-done = bf16[2048,512]{1,0:T(8,128)(2,1)} async-done(((bf16[512,512]{1,0:T(8,128)(2,1)}), bf16[2048,512]{1,0:T(8,128)(2,1)}) %all-gather.37.cloned.1.call-update) | async-done | bytes 2097168 | tf_op jit(solution)/shard_map/all_gather | solution.py:80
  1547.1 28.6 %reduce-scatter.45.cloned.1.call-done = bf16[512,512]{1,0:T(8,128)(2,1)} async-done(((bf16[2048,512]{1,0:T(8,128)(2,1)}), bf16[512,512]{1,0:T(8,128)(2,1)}) %reduce-scatter.45.cloned.1.call-update) | async-done | bytes 524304 | tf_op jit(solution)/shard_map/reduce_scatter | solution.py:122
  1576.5 36.4 %while.71 = (s32[]{:T(128)}, bf16[512,512]{1,0:T(8,128)(2,1)}, f32[2048,128]{1,0:T(8,128)S(1)}, f32[2048,128]{1,0:T(8,128)}, bf16[512,512]{1,0:T(8,128)(2,1)}, /...) while((s32[]{:T(128)}, bf16[512,512]{1,0:T(8,128)(2,1)}, ...), condition=%wide.region_59.60_spmd.clone, body=%wide.region_57.0_spmd.clone.sunk | while | flops 1355087360 | bytes 54802828 | solution.py:208
  1613.9 39.2 %while.70 = (s32[]{:T(128)}, bf16[512,512]{1,0:T(8,128)(2,1)}, f32[2048,128]{1,0:T(8,128)S(1)}, f32[2048,128]{1,0:T(8,128)}, bf16[512,512]{1,0:T(8,128)(2,1)}, /...) while((s32[]{:T(128)}, bf16[512,512]{1,0:T(8,128)(2,1)}, ...), condition=%wide.region_43.44_spmd.clone, body=%wide.region_41.0_spmd.clone.sunk | while | flops 1355087360 | bytes 54802828 | solution.py:208
  1663.0 7.7 fusion.151
  1670.8 9.3 add_convert_fusion.1
  1690.6 11.4 add_convert_fusion
  1706.5 71.6 %all-reduce.12.cloned.1.call-done = (bf16[2048,256]{1,0:T(8,128)(2,1)}, bf16[2048,256]{1,0:T(8,128)(2,1)}) async-done(((bf16[2048,256]{1,0:T(8,128)(2,1)}, bf16[2048,256]{1,0:T(8,128)(2,1)}), (bf16[2048,256]{1,0:T(8,128)(2,1)}, bf16[2048,256]{1,0:T(8,128)(2,1)})) %all-reduce.12.cloned.1.call-update) | async-done | bytes 2097168 | tf_op jit(solution)/shard_map/psum | solution.py:287
  1790.1 34.3 %reduce-scatter.47.cloned.1.call-done = bf16[512,512]{1,0:T(8,128)(2,1)} async-done(((bf16[2048,512]{1,0:T(8,128)(2,1)}), bf16[512,512]{1,0:T(8,128)(2,1)}) %reduce-scatter.47.cloned.1.call-update) | async-done | bytes 524304 | tf_op jit(solution)/shard_map/reduce_scatter | solution.py:137
  1825.9 43.9 %reduce-scatter.39.cloned.1.call-done = bf16[512,512]{1,0:T(8,128)(2,1)} async-done(((bf16[2048,512]{1,0:T(8,128)(2,1)}), bf16[512,512]{1,0:T(8,128)(2,1)}) %reduce-scatter.39.cloned.1.call-update) | async-done | bytes 524304 | tf_op jit(solution)/shard_map/reduce_scatter | solution.py:137
  1872.8 21.0 %all-reduce = (f32[512]{0:T(512)}, f32[512]{0:T(512)}, f32[512]{0:T(512)}, f32[512]{0:T(512)}) all-reduce(f32[512]{0:T(512)S(1)} %add.446, f32[512]{0:T(512)S(1)} %add.447, f32[512]{0:T(512)S(1)} %add.451, f32[512]{0:T(512)S(1)} %add.452), channel_id=1, replica_groups=mesh['dp'=2,'row'=4,'col'=4] {'dp','row'}, use_global_device_ids=true, to_apply=%region_68.69 | all-reduce | flops 2048 | bytes 16384 | tf_op jit(solution)/shard_map/psum | solution.py:314
  1903.3 107.5 %all-reduce.14.cloned.1.call-done = (bf16[512,512]{1,0:T(8,128)(2,1)}, bf16[512,256]{1,0:T(8,128)(2,1)}, bf16[512,512]{1,0:T(8,128)(2,1)}, bf16[512,2048]{1,0:T(8,128)(2,1)}, bf16[2048,512]{1,0:T(8,128)(2,1)}) async-done(((bf16[512,512]{1,0:T(8,128)(2,1)}, bf16[512,256]{1,0:T(8,128)(2,1)}, bf16[512,512]{1,0:T(8,128)(2,1)}, bf16[512,2048]{1,0:T(8,128)(2,1)}, bf16[2048,512]{1,0:T(8,128)(2,1)}), ...) | async-done | bytes 5505040 | tf_op jit(solution)/shard_map/psum | solution.py:308
  (456 shorter events, 261.8 us)
Async XLA Ops:
  7.2 507.1 %copy-start = (bf16[512,2048]{1,0:T(8,128)(2,1)S(1)}, bf16[512,2048]{1,0:T(8,128)(2,1)}, u32[]{:S(2)}) copy-start(bf16[512,2048]{1,0:T(8,128)(2,1)} %param.30) | copy-start | bytes 6291460
  7.2 63.6 %all-gather.17.cloned.1.call-start = ((), (), s32[]{:S(2)}) async-start(), calls=%async_computation.16 | async-start | bytes 2621440 | tf_op jit(solution)/shard_map/all_gather | solution.py:68
  13.0 1434.4 %copy-start.38 = (f32[512]{0:T(512)}, f32[512]{0:T(512)S(1)}, u32[]{:S(2)}) copy-start(f32[512]{0:T(512)S(1)} %get-tuple-element.914) | copy-start | bytes 6148
  13.0 1434.4 %copy-start.40 = (f32[512]{0:T(512)}, f32[512]{0:T(512)S(1)}, u32[]{:S(2)}) copy-start(f32[512]{0:T(512)S(1)} %get-tuple-element.913) | copy-start | bytes 6148
  24.4 93.2 %all-gather.25.cloned.1.call-start = ((), (), s32[]{:S(2)}) async-start(), calls=%async_computation.24 | async-start | bytes 2621440 | tf_op jit(solution)/shard_map/all_gather | solution.py:68
  25.2 225.0 %reduce-scatter.17.cloned.1.call-start = ((), (), s32[]{:S(2)}) async-start(), calls=%async_computation.17 | async-start | bytes 5242880 | tf_op jit(solution)/shard_map/reduce_scatter | solution.py:92
  75.7 196.4 %reduce-scatter.25.cloned.1.call-start = ((), (), s32[]{:S(2)}) async-start(), calls=%async_computation.25 | async-start | bytes 5242880 | tf_op jit(solution)/shard_map/reduce_scatter | solution.py:92
  122.5 171.8 %all-gather.19.cloned.1.call-start = ((), (), s32[]{:S(2)}) async-start(), calls=%async_computation.18 | async-start | bytes 2621440 | tf_op jit(solution)/shard_map/all_gather | solution.py:74
  272.0 46.2 %all-gather.27.cloned.1.call-start = ((), (), s32[]{:S(2)}) async-start(), calls=%async_computation.26 | async-start | bytes 2621440 | tf_op jit(solution)/shard_map/all_gather | solution.py:74
  294.1 70.9 %reduce-scatter.19.cloned.1.call-start = ((), (), s32[]{:S(2)}) async-start(), calls=%async_computation.19 | async-start | bytes 2621440 | tf_op jit(solution)/shard_map/reduce_scatter | solution.py:107
  298.6 112.5 %copy-start.2 = (bf16[2,512,512]{2,1,0:T(8,128)(2,1)S(1)}, bf16[2,512,512]{2,1,0:T(8,128)(2,1)}, u32[]{:S(2)}) copy-start(bf16[2,512,512]{2,1,0:T(8,128)(2,1)} %param.20) | copy-start | bytes 3145732
  298.6 112.5 %reduce-scatter.27.cloned.1.call-start = ((), (), s32[]{:S(2)}) async-start(), calls=%async_computation.27 | async-start | bytes 2621440 | tf_op jit(solution)/shard_map/reduce_scatter | solution.py:107
  322.4 97.0 %copy-start.51 = (f32[512]{0:T(512)S(1)}, f32[512]{0:T(512)}, u32[]{:S(2)}) copy-start(f32[512]{0:T(512)} %param.28) | copy-start | bytes 6148
  322.5 97.0 %copy-start.57 = (f32[512]{0:T(512)S(1)}, f32[512]{0:T(512)}, u32[]{:S(2)}) copy-start(f32[512]{0:T(512)} %param.29) | copy-start | bytes 6148
  322.5 145.1 %all-gather.33.cloned.1.call-start = ((), (), s32[]{:S(2)}) async-start(), calls=%async_computation.32 | async-start | bytes 2621440 | tf_op jit(solution)/shard_map/all_gather | solution.py:80
  422.6 91.7 %all-gather.21.cloned.1.call-start = ((), (), s32[]{:S(2)}) async-start(), calls=%async_computation.20 | async-start | bytes 2621440 | tf_op jit(solution)/shard_map/all_gather | solution.py:68
  423.2 137.9 %all-gather.41.cloned.1.call-start = ((), (), s32[]{:S(2)}) async-start(), calls=%async_computation.40 | async-start | bytes 2621440 | tf_op jit(solution)/shard_map/all_gather | solution.py:80
  423.9 183.9 %all-gather.29.cloned.1.call-start = ((), (), s32[]{:S(2)}) async-start(), calls=%async_computation.28 | async-start | bytes 2621440 | tf_op jit(solution)/shard_map/all_gather | solution.py:68
  424.5 256.3 %reduce-scatter.33.cloned.1.call-start = ((), (), s32[]{:S(2)}) async-start(), calls=%async_computation.33 | async-start | bytes 10485760 | tf_op jit(solution)/shard_map/reduce_scatter | solution.py:122
  477.6 331.9 %reduce-scatter.21.cloned.1.call-start = ((), (), s32[]{:S(2)}) async-start(), calls=%async_computation.21 | async-start | bytes 20971520 | tf_op jit(solution)/shard_map/reduce_scatter | solution.py:92
  524.3 359.5 %reduce-scatter.41.cloned.1.call-start = ((), (), s32[]{:S(2)}) async-start(), calls=%async_computation.41 | async-start | bytes 10485760 | tf_op jit(solution)/shard_map/reduce_scatter | solution.py:122
  571.2 441.4 %reduce-scatter.29.cloned.1.call-start = ((), (), s32[]{:S(2)}) async-start(), calls=%async_computation.29 | async-start | bytes 20971520 | tf_op jit(solution)/shard_map/reduce_scatter | solution.py:92
  619.3 453.6 %all-gather.23.cloned.1.call-start = ((), (), s32[]{:S(2)}) async-start(), calls=%async_computation.22 | async-start | bytes 10485760 | tf_op jit(solution)/shard_map/all_gather | solution.py:74
  816.0 317.2 %all-gather.35.cloned.1.call-start = ((), (), s32[]{:S(2)}) async-start(), calls=%async_computation.34 | async-start | bytes 10485760 | tf_op jit(solution)/shard_map/all_gather | solution.py:84
  816.6 376.5 %all-gather.43.cloned.1.call-start = ((), (), s32[]{:S(2)}) async-start(), calls=%async_computation.42 | async-start | bytes 10485760 | tf_op jit(solution)/shard_map/all_gather | solution.py:84
  1019.1 233.7 %all-gather.31.cloned.1.call-start = ((), (), s32[]{:S(2)}) async-start(), calls=%async_computation.30 | async-start | bytes 10485760 | tf_op jit(solution)/shard_map/all_gather | solution.py:74
  1019.7 279.3 %reduce-scatter.23.cloned.1.call-start = ((), (), s32[]{:S(2)}) async-start(), calls=%async_computation.23 | async-start | bytes 2621440 | tf_op jit(solution)/shard_map/reduce_scatter | solution.py:107
  1082.8 262.5 %reduce-scatter.35.cloned.1.call-start = ((), (), s32[]{:S(2)}) async-start(), calls=%async_computation.35 | async-start | bytes 2621440 | tf_op jit(solution)/shard_map/reduce_scatter | solution.py:137
  1142.4 248.9 %reduce-scatter.43.cloned.1.call-start = ((), (), s32[]{:S(2)}) async-start(), calls=%async_computation.43 | async-start | bytes 2621440 | tf_op jit(solution)/shard_map/reduce_scatter | solution.py:137
  1202.3 234.5 %copy-start.17 = (bf16[512,512]{1,0:T(8,128)(2,1)S(1)}, bf16[512,512]{1,0:T(8,128)(2,1)}, u32[]{:S(2)}) copy-start(bf16[512,512]{1,0:T(8,128)(2,1)} %reduce-scatter.19.cloned.1.call-done) | copy-start | bytes 1572868
  1202.3 234.5 %copy-start.18 = (bf16[512,512]{1,0:T(8,128)(2,1)S(1)}, bf16[512,512]{1,0:T(8,128)(2,1)}, u32[]{:S(2)}) copy-start(bf16[512,512]{1,0:T(8,128)(2,1)} %reduce-scatter.27.cloned.1.call-done) | copy-start | bytes 1572868
  1202.3 234.5 %reduce-scatter.31.cloned.1.call-start = ((), (), s32[]{:S(2)}) async-start(), calls=%async_computation.31 | async-start | bytes 2621440 | tf_op jit(solution)/shard_map/reduce_scatter | solution.py:107
  1262.7 184.8 %copy-start.19 = (bf16[2,512,512]{2,1,0:T(8,128)(2,1)S(1)}, bf16[2,512,512]{2,1,0:T(8,128)(2,1)}, u32[]{:S(2)}) copy-start(bf16[2,512,512]{2,1,0:T(8,128)(2,1)} %param.22) | copy-start | bytes 3145732
  1262.7 233.2 %all-gather.45.cloned.1.call-start = ((), (), s32[]{:S(2)}) async-start(), calls=%async_computation.44 | async-start | bytes 2621440 | tf_op jit(solution)/shard_map/all_gather | solution.py:80
  1450.9 91.7 %all-gather.37.cloned.1.call-start = ((), (), s32[]{:S(2)}) async-start(), calls=%async_computation.36 | async-start | bytes 2621440 | tf_op jit(solution)/shard_map/all_gather | solution.py:80
  1451.5 91.1 %copy-start.65 = (bf16[512,512]{1,0:T(8,128)(2,1)S(1)}, bf16[512,512]{1,0:T(8,128)(2,1)}, u32[]{:S(2)}) copy-start(bf16[512,512]{1,0:T(8,128)(2,1)} %param.27) | copy-start | bytes 1572868
  1451.5 124.2 %reduce-scatter.45.cloned.1.call-start = ((), (), s32[]{:S(2)}) async-start(), calls=%async_computation.45 | async-start | bytes 2621440 | tf_op jit(solution)/shard_map/reduce_scatter | solution.py:122
  1500.2 112.9 %reduce-scatter.37.cloned.1.call-start = ((), (), s32[]{:S(2)}) async-start(), calls=%async_computation.37 | async-start | bytes 2621440 | tf_op jit(solution)/shard_map/reduce_scatter | solution.py:122
  1546.8 111.8 %all-gather.47.cloned.1.call-start = ((), (), s32[]{:S(2)}) async-start(), calls=%async_computation.46 | async-start | bytes 2621440 | tf_op jit(solution)/shard_map/all_gather | solution.py:84
  1613.0 73.2 %all-gather.39.cloned.1.call-start = ((), (), s32[]{:S(2)}) async-start(), calls=%async_computation.38 | async-start | bytes 2621440 | tf_op jit(solution)/shard_map/all_gather | solution.py:84
  1653.1 124.9 %all-reduce.12.cloned.1.call-start = ((), (), s32[]{:S(2)}) async-start(), calls=%async_computation.48 | async-start | bytes 4194304 | tf_op jit(solution)/shard_map/psum | solution.py:287
  1658.1 166.3 %reduce-scatter.47.cloned.1.call-start = ((), (), s32[]{:S(2)}) async-start(), calls=%async_computation.47 | async-start | bytes 2621440 | tf_op jit(solution)/shard_map/reduce_scatter | solution.py:137
  1663.0 206.8 %reduce-scatter.39.cloned.1.call-start = ((), (), s32[]{:S(2)}) async-start(), calls=%async_computation.39 | async-start | bytes 2621440 | tf_op jit(solution)/shard_map/reduce_scatter | solution.py:137
  1690.4 320.3 %all-reduce.14.cloned.1.call-start = ((), (), s32[]{:S(2)}) async-start(), calls=%async_computation.49 | async-start | bytes 11010048 | tf_op jit(solution)/shard_map/psum | solution.py:308
  1787.9 81.9 %copy-start.3 = (bf16[2,512,512]{2,1,0:T(8,128)(2,1)S(1)}, bf16[2,512,512]{2,1,0:T(8,128)(2,1)}, u32[]{:S(2)}) copy-start(bf16[2,512,512]{2,1,0:T(8,128)(2,1)} %param.20) | copy-start | bytes 3145732
  1787.9 81.9 %copy-start.41 = (f32[512]{0:T(512)S(1)}, f32[512]{0:T(512)}, u32[]{:S(2)}) copy-start(f32[512]{0:T(512)} %copy-done.40) | copy-start | bytes 6148
  1787.9 81.9 %copy-start.44 = (f32[512]{0:T(512)S(1)}, f32[512]{0:T(512)}, u32[]{:S(2)}) copy-start(f32[512]{0:T(512)} %copy-done.43) | copy-start | bytes 6148
  1790.1 109.9 %copy-start.20 = (f32[512,512]{1,0:T(8,128)S(1)}, f32[512,512]{1,0:T(8,128)}, u32[]{:S(2)}) copy-start(f32[512,512]{1,0:T(8,128)} %get-tuple-element.869) | copy-start | bytes 3145732
  (90 other events, 1114.5 us)
Sparse Core Ops, SparseCore 0:
  24.5 46.2 all-gather.16
  72.9 44.6 all-gather.24
  120.7 65.8 reduce-scatter.16
  189.7 61.9 reduce-scatter.24
  272.1 21.4 all-gather.18
  295.6 22.5 all-gather.26
  321.1 43.8 reduce-scatter.18
  367.9 43.1 reduce-scatter.26
  422.7 44.8 all-gather.32
  469.6 44.6 all-gather.20
  516.4 44.6 all-gather.40
  563.1 44.6 all-gather.28
  610.4 70.3 reduce-scatter.32
  683.4 126.0 reduce-scatter.20
  812.0 71.7 reduce-scatter.40
  886.4 126.1 reduce-scatter.28
  1014.5 58.2 all-gather.22
  1074.9 58.2 all-gather.34
  1134.8 58.2 all-gather.42
  1194.5 58.2 all-gather.30
  1255.1 43.8 reduce-scatter.22
  1302.0 43.1 reduce-scatter.34
  1348.1 43.1 reduce-scatter.42
  1393.6 43.1 reduce-scatter.30
  1451.0 44.8 all-gather.44
  1497.9 44.6 all-gather.36
  1545.5 30.1 reduce-scatter.44
  1579.0 31.4 reduce-scatter.36
  1613.1 22.5 all-gather.46
  1653.2 22.5 all-gather.38
  1680.1 97.9 all-reduce.11
  1781.0 43.3 reduce-scatter.46
  1826.6 43.1 reduce-scatter.38
  1873.5 137.2 all-reduce.13
where the time goes:
time: 2040 us; the launch traced here: 2030 us
  waiting for transfers between devices  1490 us (73%)
  matrix products  265 us (13%)
  blocking collectives  165 us (8%)
  other arithmetic  67.9 us (3%)
  local copies, waits for them, and re-layouts  23 us (1%)
    reduce_scatter x4, waiting for transfers between devices, reduce_cols(): lax.psum_scatter(partial_term(jnp.int32(0), lax.axis_size('col') * (left_...  258 us
    reduce_scatter x4, waiting for transfers between devices, reduce_grad_rows(): lax.psum_scatter(partial_term(jnp.int32(0), left_side.shape[0] // lax.axi...  170 us
    reduce_scatter x4, waiting for transfers between devices, reduce_rows(): lax.psum_scatter(partial_term(jnp.int32(0), left_side.shape[0] // lax.axi...  170 us
    all_gather x4, waiting for transfers between devices, gather_grad_rows(): return lax.all_gather(hidden, 'row', axis=0, tiled=True)  166 us
    all_gather x4, waiting for transfers between devices, gather_rows(): return lax.all_gather(hidden, 'row', axis=0, tiled=True)  159 us
    reduce_scatter x4, waiting for transfers between devices, reduce_grad_cols(): lax.psum_scatter(partial_term(jnp.int32(0), left_side.shape[0] // lax.axi...  157 us
    all_gather x4, waiting for transfers between devices, gather_cols(): lax.all_gather(as_sent(hidden), 'col', axis=0, tiled=True)  123 us
    psum x1, blocking collectives, local(): lax.psum(jnp.dot(gathered_one, kv_weight, preferred_element_type=jnp.floa...  116 us
  transfers between devices with their start and end apart: 34, of which 28 were waited for; matrix products, arithmetic and copies ran while one was open for 15% of the time, Pallas kernels for 0%

commit v1 on v0

v1 whole, which is shorter than its diff:
```python
import jax
import jax.numpy as jnp
from jax import lax
from jax.sharding import PartitionSpec as P

eps = 1e-05
BF = jnp.bfloat16
F32 = jnp.float32


def mm(a, b, ca, cb):
    return lax.dot_general(a, b, (((ca,), (cb,)), ((), ())), preferred_element_type=F32)


def norm_stats(hidden):
    centre = jnp.mean(hidden, axis=1, keepdims=True)
    spread = jnp.mean(hidden * hidden, axis=1, keepdims=True) - centre * centre
    return centre, lax.rsqrt(spread + eps)


def norm_apply(hidden, centre, inverse, gain, bias, keep):
    return (keep * ((hidden - centre) * inverse * gain + bias)).astype(BF)


def norm_backward(gradient, normed, inverse, gain, keep):
    masked = keep * gradient
    scaled = masked * gain
    first = jnp.mean(scaled, axis=1, keepdims=True)
    second = jnp.mean(scaled * normed, axis=1, keepdims=True)
    result = inverse * (scaled - first - normed * second)
    return result, jnp.sum(masked * normed, axis=0), jnp.sum(masked, axis=0)


def turn(weight):
    return lax.all_to_all(weight, "col", 0, 1, tiled=True)


def turn_back(rows):
    return lax.all_to_all(rows, "col", 1, 0, tiled=True)


def gather(x, axes, dim=0):
    return lax.all_gather(x, axes, axis=dim, tiled=True)


def scatter(x, axes):
    return lax.psum_scatter(x, axes, scatter_dimension=0, tiled=True)


def pairs_allowed(first, count, keys, length):
    q = first + jnp.arange(count, dtype=jnp.int32)[:, None]
    k = jnp.arange(keys, dtype=jnp.int32)[None, :]
    return (k <= q) & (k < length)


def attend(queries, kv, lengths, first):
    b, t, width = queries.shape
    hd = kv.shape[2] // 2
    outs, logs = [], []
    for s in range(b):
        keys, values = kv[s, :, :hd], kv[s, :, hd:]
        allowed = pairs_allowed(first, t, kv.shape[1], lengths[s])
        for h in range(width // hd):
            q = queries[s, :, h * hd : (h + 1) * hd]
            scores = jnp.where(allowed, mm(q, keys, 1, 1) * hd**-0.5, -jnp.inf)
            top = jnp.max(scores, axis=1, keepdims=True)
            log_total = top + jnp.log(jnp.sum(jnp.exp(scores - top), axis=1, keepdims=True))
            weights = jnp.exp(scores - log_total).astype(BF)
            outs.append(mm(weights, values, 1, 0).astype(BF))
            logs.append(log_total)
    n = width // hd
    out = jnp.stack([jnp.concatenate(outs[s * n : (s + 1) * n], axis=1) for s in range(b)])
    log = jnp.stack([jnp.concatenate(logs[s * n : (s + 1) * n], axis=1) for s in range(b)])
    return out, log


def attend_back(queries, kv, lengths, first, logs, grad):
    b, t, width = queries.shape
    hd = kv.shape[2] // 2
    scale = hd**-0.5
    dqs, dkvs = [], []
    for s in range(b):
        keys, values = kv[s, :, :hd], kv[s, :, hd:]
        allowed = pairs_allowed(first, t, kv.shape[1], lengths[s])
        dk = dv = 0.0
        dq = []
        for h in range(width // hd):
            q = queries[s, :, h * hd : (h + 1) * hd]
            g = grad[s, :, h * hd : (h + 1) * hd]
            scores = jnp.where(allowed, mm(q, keys, 1, 1) * scale, -jnp.inf)
            p = jnp.exp(scores - logs[s, :, h : h + 1])
            dp = mm(g, values, 1, 1)
            ds = (p * (dp - jnp.sum(p * dp, axis=1, keepdims=True))).astype(BF)
            dq.append((mm(ds, keys, 1, 0) * scale).astype(BF))
            dk = dk + mm(ds, q, 0, 0) * scale
            dv = dv + mm(p.astype(BF), g, 0, 0)
        dqs.append(jnp.concatenate(dq, axis=1))
        dkvs.append(jnp.concatenate([dk, dv], axis=1).astype(BF))
    return jnp.stack(dqs), jnp.stack(dkvs)


def local(
    tokens,
    lengths,
    cotangent,
    norm1_gain,
    norm1_bias,
    query_weight,
    kv_weight,
    out_weight,
    norm2_gain,
    norm2_bias,
    up_weight,
    down_weight,
):
    b, t, f = tokens.shape
    nd, nr, nc = (lax.axis_size(a) for a in ("dp", "row", "col"))
    dp, row, col = (lax.axis_index(a) for a in ("dp", "row", "col"))
    m, d = b * t, f * nc
    own = m // nc
    hd = kv_weight.shape[1] // 2
    plane = ("dp", "col")

    slot = row * t + jnp.arange(t, dtype=jnp.int32)
    keep = (slot[None, :] < lengths[:, None]).astype(F32).reshape(m, 1)

    def mine(x):
        return lax.dynamic_slice_in_dim(x, col * own, own, 0)

    def half(w):
        n = w.shape[0] // nd
        return lax.dynamic_slice_in_dim(w, dp * n, n, 0)

    wq = gather(turn(query_weight.T), "row")
    wo = gather(turn(out_weight), "row")
    wu = gather(turn(half(up_weight.T)), "row")
    wd = gather(turn(half(down_weight)), "row")
    wkv = gather(kv_weight, "col")
    vectors = gather(jnp.stack([norm1_gain, norm1_bias, norm2_gain, norm2_bias]), "col", 1)
    gain1, bias1, gain2, bias2 = (vectors[i : i + 1] for i in range(4))

    x = gather(tokens.reshape(m, f), "col", 1)
    grad_final = (keep * cotangent.reshape(m, f).astype(F32)).astype(BF)
    grad_own = turn(grad_final)
    grad_all = gather(grad_own, plane)

    keep_own = mine(keep)
    centre, inverse = norm_stats(x.astype(F32))
    one = norm_apply(x.astype(F32), centre, inverse, gain1, bias1, keep)
    one_own = mine(one)
    queries = mm(one, wq, 1, 1).astype(BF).reshape(b, t, -1)
    kv_own = mm(one_own, wkv, 1, 0).astype(BF)
    kv = gather(kv_own, ("row", "col")).reshape(nr, b, t, 2 * hd)
    kv = kv.transpose(1, 0, 2, 3).reshape(b, nr * t, 2 * hd)
    attended, logs = attend(queries, kv, lengths, row * t)
    attended = attended.reshape(m, -1)
    x_own = mine(x).astype(F32)
    middle = x_own + scatter(mm(attended, wo, 1, 0).astype(BF), "col").astype(F32)

    centre2, inverse2 = norm_stats(middle)
    two_own = norm_apply(middle, centre2, inverse2, gain2, bias2, keep_own)
    two = gather(two_own, plane)
    sums = mm(two, wu, 1, 1)
    activated, pull = jax.vjp(lambda v: jax.nn.gelu(v, approximate=True), sums)
    activated = activated.astype(BF)
    ffn = scatter(mm(activated, wd, 1, 0).astype(BF), plane)
    out = turn_back((keep_own * (middle + ffn.astype(F32))).astype(BF))

    grad_act = mm(grad_all, wd, 1, 1)
    grad_up = pull(grad_act)[0].astype(BF)
    d_down = scatter(mm(activated, grad_all, 0, 0).astype(BF), "row")
    d_up = scatter(mm(grad_up, two, 0, 0).astype(BF), "row")
    e_two = scatter(mm(grad_up, wu, 1, 0).astype(BF), plane).astype(F32)
    normed2 = (middle - centre2) * inverse2
    back_two, g_gain2, g_bias2 = norm_backward(e_two, normed2, inverse2, gain2, keep_own)
    grad_middle = grad_own.astype(F32) + back_two

    grad_attn = gather(grad_middle.astype(BF), "col")
    grad_att = mm(grad_attn, wo, 1, 1).astype(BF)
    d_out = scatter(mm(attended, grad_attn, 0, 0).astype(BF), "row")
    dq, dkv = attend_back(queries, kv, lengths, row * t, logs, grad_att.reshape(b, t, -1))
    dq = dq.reshape(m, -1)
    dkv = dkv.reshape(b, nr, t, 2 * hd).transpose(1, 0, 2, 3).reshape(nr * m, 2 * hd)
    dkv_own = scatter(dkv, ("row", "col"))
    d_query = scatter(mm(dq, one, 0, 0).astype(BF), "row")
    e_one = scatter(mm(dq, wq, 1, 0).astype(BF), "col").astype(F32) + mm(dkv_own, wkv, 1, 1)
    normed1 = (x_own - mine(centre)) * mine(inverse)
    back_one, g_gain1, g_bias1 = norm_backward(e_one, normed1, mine(inverse), gain1, keep_own)
    grad_in = turn_back((grad_middle + back_one).astype(BF))

    d_kv = scatter(mm(one_own, dkv_own, 0, 0).astype(BF), "col")
    d_kv = lax.psum(d_kv, ("dp", "row")).astype(F32)
    small = lax.psum(jnp.stack([g_gain1, g_bias1, g_gain2, g_bias2]), ("dp", "row", "col"))
    small = lax.dynamic_slice_in_dim(small, col * f, f, 1)
    d_query = lax.psum(turn_back(d_query), "dp").astype(F32).T
    d_out = lax.psum(turn_back(d_out), "dp").astype(F32)
    d_up = gather(turn_back(d_up), "dp").astype(F32).T
    d_down = gather(turn_back(d_down), "dp").astype(F32)
    return (
        out.reshape(b, t, f),
        grad_in.reshape(b, t, f),
        small[0],
        small[1],
        d_query,
        d_kv,
        d_out,
        small[2],
        small[3],
        d_up,
        d_down,
    )


def solution(mesh):
    act, vec = P("dp", "row", "col"), P("col")
    wide, tall = P("col", "row"), P("row", "col")
    return jax.shard_map(
        local,
        mesh=mesh,
        in_specs=(act, P("dp"), act, vec, vec, wide, P("col", None), tall, vec, vec, wide, tall),
        out_specs=(act, act, vec, vec, wide, P("col", None), tall, vec, vec, wide, tall),
        check_vma=False,
    )
```

time: 2040 us -> 1480 us (0.73)
  waiting for transfers between devices: 1490 us -> 955 us
  matrix products: 265 us -> 215 us
    reduce_scatter x16 -> x10, waiting for transfers between devices: 756 us -> 391 us  [scatter(): return lax.psum_scatter(x, axes, scatter_dimension=0, tiled=True)]
    psum x6 -> x1, blocking collectives: 165 us -> 39.5 us  [local(): lax.psum(jnp.stack([g_gain1, g_bias1, g_gain2, g_bias2]), ('dp', 'row', '...]
    all_to_all x0 -> x6, blocking collectives: none -> 110 us  [the longest x4 75.5 us: turn(): return lax.all_to_all(weight, 'col', 0, 1, tiled=True)]
    all_gather x16 -> x12, waiting for transfers between devices: 549 us -> 445 us  [gather(): return lax.all_gather(x, axes, axis=dim, tiled=True)]
    psum x2, waiting for transfers between devices: 179 us -> 110 us  [the longest x1 69.8 us: local(): d_kv = lax.psum(d_kv, ('dp', 'row')).astype(F32)]
    dot_general x86 -> x63, matrix products: 265 us -> 215 us  [mm(): lax.dot_general(a, b, (((ca,), (cb,)), ((), ())), preferred_element_type=...]
    convert_element_type x21 -> x17, other arithmetic: 42.7 us -> 49.3 us  [the longest x8 22.4 us: attend_back(): ds = (p * (dp - jnp.sum(p * dp, axis=1, keepdims=True))).astype(BF)]
  transfers between devices with their start and end apart: 34 -> 29, of which waited for: 28 -> 24; matrix products, arithmetic and copies ran while one was open for 15% -> 13% of each run, Pallas kernels for 0% -> 0%
where the time goes in v1:
time: 1480 us
  waiting for transfers between devices  955 us (65%)
  matrix products  215 us (15%)
  blocking collectives  155 us (10%)
  other arithmetic  73.4 us (5%)
  local copies, waits for them, and re-layouts  43.2 us (3%)
  starting transfers between devices  20.1 us (1%)
  between operations  15.8 us (1%)
    all_gather x12, waiting for transfers between devices, gather(): return lax.all_gather(x, axes, axis=dim, tiled=True)  445 us
    reduce_scatter x10, waiting for transfers between devices, scatter(): return lax.psum_scatter(x, axes, scatter_dimension=0, tiled=True)  391 us
    dot_general x63, matrix products, mm(): lax.dot_general(a, b, (((ca,), (cb,)), ((), ())), preferred_element_type=...  215 us
    all_to_all x4, blocking collectives, turn(): return lax.all_to_all(weight, 'col', 0, 1, tiled=True)  75.5 us
    psum x1, waiting for transfers between devices, local(): d_kv = lax.psum(d_kv, ('dp', 'row')).astype(F32)  69.8 us
    psum x1, waiting for transfers between devices, local(): d_query = lax.psum(turn_back(d_query), 'dp').astype(F32).T  40.7 us
    psum x1, blocking collectives, local(): lax.psum(jnp.stack([g_gain1, g_bias1, g_gain2, g_bias2]), ('dp', 'row', '...  39.5 us
    all_to_all x2, blocking collectives, turn_back(): return lax.all_to_all(rows, 'col', 1, 0, tiled=True)  34.6 us
  transfers between devices with their start and end apart: 29, of which 24 were waited for; matrix products, arithmetic and copies ran while one was open for 13% of the time, Pallas kernels for 0%

profile of v1, /device:TPU:0, one launch (start us, length us, event | category | flops | bytes accessed | tf_op | source)
XLA Modules:
  0.0 1477.2 jit_solution(9713727474657189356)
XLA Ops:
  10.0 13.0 all_to_all.200
  24.2 5.3 all_gather.40
  29.6 17.6 %all-gather.13.cloned.1.call-done = bf16[1024,2048]{1,0:T(8,128)(2,1)} async-done(((bf16[1024,512]{1,0:T(8,128)(2,1)}), bf16[1024,2048]{1,0:T(8,128)(2,1)}) %all-gather.13.cloned.1.call-update) | async-done | bytes 4194320 | tf_op jit(solution)/shard_map/all_gather | solution.py:43
  50.8 7.5 fusion.11
  58.3 7.5 all-gather.17.cloned.1.call-done
  73.9 6.9 all-to-all-done.1
  82.0 32.2 %all-gather.15.cloned.1.call-done = bf16[512,2048]{0,1:T(8,128)(2,1)} async-done(((bf16[128,2048]{0,1:T(8,128)(2,1)}), bf16[512,2048]{0,1:T(8,128)(2,1)}) %all-gather.15.cloned.1.call-update) | async-done | bytes 2097168 | tf_op jit(solution)/shard_map/all_gather | solution.py:43
  114.2 5.2 convolution_convert_fusion.10
  119.4 37.1 %all-gather.19.cloned.1.call-done = bf16[4096,256]{1,0:T(8,128)(2,1)} async-done(((bf16[256,256]{1,0:T(8,128)(2,1)}), bf16[4096,256]{1,0:T(8,128)(2,1)}) %all-gather.19.cloned.1.call-update) | async-done | bytes 2097168 | tf_op jit(solution)/shard_map/all_gather | solution.py:43
  184.7 18.8 %all-gather.21.cloned.1.call-done = bf16[512,2048]{0,1:T(8,128)(2,1)} async-done(((bf16[128,2048]{0,1:T(8,128)(2,1)}), bf16[512,2048]{0,1:T(8,128)(2,1)}) %all-gather.21.cloned.1.call-update) | async-done | bytes 2097168 | tf_op jit(solution)/shard_map/all_gather | solution.py:43
  203.5 6.3 convolution_convert_fusion.5
  210.0 17.2 %all_to_all.201 = bf16[4,256,512]{2,1,0:T(8,128)(2,1)S(1)} all-to-all(bf16[4,256,512]{2,1,0:T(8,128)(2,1)S(1)} %bitcast.406), channel_id=1, replica_groups=mesh['dp'=2,'row'=4,'col'=4] {'col'}, dimensions={0} | all-to-all | bytes 2097152 | tf_op jit(solution)/shard_map/all_to_all | solution.py:35
  229.1 28.4 %all_to_all.202 = bf16[4,256,512]{2,1,0:T(8,128)(2,1)S(1)} all-to-all(bf16[4,256,512]{2,1,0:T(8,128)(2,1)S(1)} %fusion.58), channel_id=1, replica_groups=mesh['dp'=2,'row'=4,'col'=4] {'col'}, dimensions={0} | all-to-all | bytes 2097152 | tf_op jit(solution)/shard_map/all_to_all | solution.py:35
  260.6 16.9 %all_to_all.203 = bf16[4,256,512]{2,1,0:T(8,128)(2,1)S(1)} all-to-all(bf16[4,256,512]{2,1,0:T(8,128)(2,1)S(1)} %bitcast.413), channel_id=1, replica_groups=mesh['dp'=2,'row'=4,'col'=4] {'col'}, dimensions={0} | all-to-all | bytes 2097152 | tf_op jit(solution)/shard_map/all_to_all | solution.py:35
  284.8 62.0 %all-gather.27.cloned.1.call-done = bf16[1024,2048]{0,1:T(8,128)(2,1)} async-done(((bf16[256,2048]{0,1:T(8,128)(2,1)}), bf16[1024,2048]{0,1:T(8,128)(2,1)}) %all-gather.27.cloned.1.call-update) | async-done | bytes 4194320 | tf_op jit(solution)/shard_map/all_gather | solution.py:43
  346.8 55.2 %all-gather.29.cloned.1.call-done = bf16[2048,2048]{1,0:T(8,128)(2,1)} async-done(((bf16[256,2048]{1,0:T(8,128)(2,1)}), bf16[2048,2048]{1,0:T(8,128)(2,1)}) %all-gather.29.cloned.1.call-update) | async-done | bytes 8388624 | tf_op jit(solution)/shard_map/all_gather | solution.py:43
  402.0 14.5 fusion.125
  416.4 67.8 %all-gather.25.cloned.1.call-done = bf16[1024,2048]{0,1:T(8,128)(2,1)} async-done(((bf16[256,2048]{0,1:T(8,128)(2,1)}), bf16[1024,2048]{0,1:T(8,128)(2,1)}) %all-gather.25.cloned.1.call-update) | async-done | bytes 4194320 | tf_op jit(solution)/shard_map/all_gather | solution.py:43
  484.2 55.1 %all-gather.23.cloned.1.call-done = bf16[2048,2048]{1,0:T(8,128)(2,1)} async-done(((bf16[256,2048]{1,0:T(8,128)(2,1)}), bf16[2048,2048]{1,0:T(8,128)(2,1)}) %all-gather.23.cloned.1.call-update) | async-done | bytes 8388624 | tf_op jit(solution)/shard_map/all_gather | solution.py:43
  539.3 22.2 %fusion.6 = (bf16[2048,1024]{1,0:T(8,128)(2,1)S(1)}, f32[2048,1024]{1,0:T(8,128)}) fusion(f32[2048,1024]{1,0:T(8,128)} %fusion.125, bf16[2048,2048]{1,0:T(8,128)(2,1)} %all-gather.23.cloned.1.call-done, bf16[1024,2048]{0,1:T(8,128)(2,1)} %all-gather.25.cloned.1.call-done), kind=kOutput, calls=%fused_computation.11 | convolution fusion | flops 8631877632 | bytes 33554432 | tf_op jit(solution)/shard_map/dot_general | solution.py:12
  563.4 11.0 convolution_convert_fusion
  574.5 15.6 %convolution_convert_fusion.1 = bf16[2048,2048]{1,0:T(8,128)(2,1)} fusion(bf16[1024,2048]{0,1:T(8,128)(2,1)} %all-gather.27.cloned.1.call-done, f32[2048,1024]{1,0:T(8,128)} %get-tuple-element.69), kind=kOutput, calls=%fused_computation.20 | convolution fusion | flops 8613003264 | bytes 20971520 | tf_op jit(solution)/shard_map/dot_general | solution.py:12
  590.2 55.7 %reduce-scatter.15.cloned.1.call-done = bf16[256,2048]{1,0:T(8,128)(2,1)} async-done(((bf16[2048,2048]{1,0:T(8,128)(2,1)}), bf16[256,2048]{1,0:T(8,128)(2,1)}) %reduce-scatter.15.cloned.1.call-update) | async-done | bytes 1048592 | tf_op jit(solution)/shard_map/reduce_scatter | solution.py:47
  648.7 71.9 %reduce-scatter.13.cloned.1.call-done = bf16[256,2048]{1,0:T(8,128)(2,1)} async-done(((bf16[2048,2048]{1,0:T(8,128)(2,1)}), bf16[256,2048]{1,0:T(8,128)(2,1)}) %reduce-scatter.13.cloned.1.call-update) | async-done | bytes 1048592 | tf_op jit(solution)/shard_map/reduce_scatter | solution.py:47
  720.5 5.3 fusion.111
  725.9 34.5 %all-gather.31.cloned.1.call-done = bf16[1024,2048]{1,0:T(8,128)(2,1)} async-done(((bf16[256,2048]{1,0:T(8,128)(2,1)}), bf16[1024,2048]{1,0:T(8,128)(2,1)}) %all-gather.31.cloned.1.call-update) | async-done | bytes 4194320 | tf_op jit(solution)/shard_map/all_gather | solution.py:43
  760.4 5.3 convolution_convert_fusion.9
  804.8 4.4 multiply_convert_fusion.4
  812.1 4.4 multiply_convert_fusion.8
  849.0 16.0 %convolution_convert_fusion.2 = bf16[1024,2048]{1,0:T(8,128)(2,1)} fusion(bf16[2048,2048]{1,0:T(8,128)(2,1)} %all-gather.29.cloned.1.call-done, f32[2048,1024]{1,0:T(8,128)} %get-tuple-element.69), kind=kOutput, calls=%fused_computation.73 | convolution fusion | flops 8610906112 | bytes 20971520 | tf_op jit(solution)/shard_map/dot_general | solution.py:12
  865.5 14.2 convolution_convert_fusion.3
  892.4 6.0 convolution_convert_fusion.7
  898.6 5.9 convolution_convert_fusion.6
  904.5 6.2 reduce-scatter.19.cloned.1.call-done
  913.5 75.8 %reduce-scatter.29.cloned.1.call-done = bf16[256,2048]{1,0:T(8,128)(2,1)} async-done(((bf16[1024,2048]{1,0:T(8,128)(2,1)}), bf16[256,2048]{1,0:T(8,128)(2,1)}) %reduce-scatter.29.cloned.1.call-update) | async-done | bytes 1048592 | tf_op jit(solution)/shard_map/reduce_scatter | solution.py:47
  990.6 17.6 %all_to_all.204 = bf16[256,4,512]{2,0,1:T(8,128)(2,1)} all-to-all(bf16[256,4,512]{2,0,1:T(8,128)(2,1)S(1)} %bitcast.415), channel_id=1, replica_groups=mesh['dp'=2,'row'=4,'col'=4] {'col'}, dimensions={1} | all-to-all | bytes 2097152 | tf_op jit(solution)/shard_map/all_to_all | solution.py:39
  1008.3 6.0 convolution_convert_fusion.4
  1014.3 54.5 %reduce-scatter.27.cloned.1.call-done = bf16[256,2048]{1,0:T(8,128)(2,1)} async-done(((bf16[1024,2048]{1,0:T(8,128)(2,1)}), bf16[256,2048]{1,0:T(8,128)(2,1)}) %reduce-scatter.27.cloned.1.call-update) | async-done | bytes 1048592 | tf_op jit(solution)/shard_map/reduce_scatter | solution.py:47
  1070.1 17.0 %all_to_all.205 = bf16[256,4,512]{2,0,1:T(8,128)(2,1)S(1)} all-to-all(bf16[256,4,512]{2,0,1:T(8,128)(2,1)S(1)} %bitcast.416), channel_id=1, replica_groups=mesh['dp'=2,'row'=4,'col'=4] {'col'}, dimensions={1} | all-to-all | bytes 2097152 | tf_op jit(solution)/shard_map/all_to_all | solution.py:39
  1088.5 26.9 %reduce-scatter.21.cloned.1.call-done = bf16[128,2048]{1,0:T(8,128)(2,1)} async-done(((bf16[512,2048]{1,0:T(8,128)(2,1)}), bf16[128,2048]{1,0:T(8,128)(2,1)}) %reduce-scatter.21.cloned.1.call-update) | async-done | bytes 524304 | tf_op jit(solution)/shard_map/reduce_scatter | solution.py:47
  1120.7 40.1 %reduce-scatter.25.cloned.1.call-done = bf16[128,2048]{1,0:T(8,128)(2,1)} async-done(((bf16[512,2048]{1,0:T(8,128)(2,1)}), bf16[128,2048]{1,0:T(8,128)(2,1)}) %reduce-scatter.25.cloned.1.call-update) | async-done | bytes 524304 | tf_op jit(solution)/shard_map/reduce_scatter | solution.py:47
  1166.3 21.9 %reduce-scatter.23.cloned.1.call-done = bf16[512,256]{1,0:T(8,128)(2,1)} async-done(((bf16[2048,256]{1,0:T(8,128)(2,1)}), bf16[512,256]{1,0:T(8,128)(2,1)}) %reduce-scatter.23.cloned.1.call-update) | async-done | bytes 262160 | tf_op jit(solution)/shard_map/reduce_scatter | solution.py:47
  1189.7 33.1 %all-gather.35.cloned.1.call-done = bf16[2048,512]{1,0:T(8,128)(2,1)} async-done(((bf16[1024,512]{1,0:T(8,128)(2,1)}), bf16[2048,512]{1,0:T(8,128)(2,1)}) %all-gather.35.cloned.1.call-update) | async-done | bytes 2097168 | tf_op jit(solution)/shard_map/all_gather | solution.py:43
  1233.3 37.7 %reduce-scatter.17.cloned.1.call-done = bf16[256,2048]{1,0:T(8,128)(2,1)} async-done(((bf16[1024,2048]{1,0:T(8,128)(2,1)}), bf16[256,2048]{1,0:T(8,128)(2,1)}) %reduce-scatter.17.cloned.1.call-update) | async-done | bytes 1048592 | tf_op jit(solution)/shard_map/reduce_scatter | solution.py:47
  1281.5 24.4 %all-gather.33.cloned.1.call-done = bf16[2048,512]{0,1:T(8,128)(2,1)} async-done(((bf16[1024,512]{0,1:T(8,128)(2,1)}), bf16[2048,512]{0,1:T(8,128)(2,1)}) %all-gather.33.cloned.1.call-update) | async-done | bytes 2097168 | tf_op jit(solution)/shard_map/all_gather | solution.py:43
  1310.2 69.8 %all-reduce.4.cloned.1.call-done = bf16[512,256]{1,0:T(8,128)(2,1)} async-done(((bf16[512,256]{1,0:T(8,128)(2,1)}), bf16[512,256]{1,0:T(8,128)(2,1)}) %all-reduce.4.cloned.1.call-update) | async-done | bytes 262160 | tf_op jit(solution)/shard_map/psum | solution.py:192
  1381.7 40.7 %all-reduce.6.cloned.1.call-done = (bf16[512,512]{1,0:T(8,128)(2,1)}, bf16[512,512]{1,0:T(8,128)(2,1)}) async-done(((bf16[512,512]{1,0:T(8,128)(2,1)}, bf16[512,512]{1,0:T(8,128)(2,1)}), (bf16[512,512]{1,0:T(8,128)(2,1)}, bf16[512,512]{1,0:T(8,128)(2,1)})) %all-reduce.6.cloned.1.call-update) | async-done | bytes 1048592 | tf_op jit(solution)/shard_map/psum | solution.py:195
  1426.7 39.5 %psum.28 = f32[4,2048]{1,0:T(4,128)S(1)} all-reduce(f32[4,2048]{1,0:T(4,128)S(1)} %pad_maximum_fusion.2), channel_id=1, replica_groups=mesh['dp'=2,'row'=4,'col'=4] {'dp','row','col'}, use_global_device_ids=true, to_apply=%region_41.42 | all-reduce | flops 8192 | bytes 65536 | tf_op jit(solution)/shard_map/psum | solution.py:193
  (320 shorter events, 203.8 us)
Async XLA Ops:
  7.2 202.7 %copy-start = (bf16[2048,512]{1,0:T(8,128)(2,1)S(1)}, bf16[2048,512]{1,0:T(8,128)(2,1)}, u32[]{:S(2)}) copy-start(bf16[2048,512]{1,0:T(8,128)(2,1)} %param.23) | copy-start | bytes 6291460
  7.2 16.9 %copy-start.53 = (s32[2]{0:T(128)S(1)}, s32[2]{0:T(128)}, u32[]{:S(2)}) copy-start(s32[2]{0:T(128)} %param.13) | copy-start | bytes 28
  7.2 17.0 %copy-start.54 = (f32[512]{0:T(512)S(1)}, f32[512]{0:T(512)}, u32[]{:S(2)}) copy-start(f32[512]{0:T(512)} %param.21) | copy-start | bytes 6148
  7.2 17.0 %copy-start.55 = (f32[512]{0:T(512)S(1)}, f32[512]{0:T(512)}, u32[]{:S(2)}) copy-start(f32[512]{0:T(512)} %param.20) | copy-start | bytes 6148
  7.2 17.0 %copy-start.56 = (f32[512]{0:T(512)S(1)}, f32[512]{0:T(512)}, u32[]{:S(2)}) copy-start(f32[512]{0:T(512)} %param.16) | copy-start | bytes 6148
  7.2 17.0 %copy-start.57 = (f32[512]{0:T(512)S(1)}, f32[512]{0:T(512)}, u32[]{:S(2)}) copy-start(f32[512]{0:T(512)} %param.15) | copy-start | bytes 6148
  7.2 39.9 %all-gather.13.cloned.1.call-start = ((), (), s32[]{:S(2)}) async-start(), calls=%async_computation.21 | async-start | bytes 5242880 | tf_op jit(solution)/shard_map/all_gather | solution.py:43
  8.0 57.8 %all-gather.17.cloned.1.call-start = ((), (), s32[]{:S(2)}) async-start(), calls=%async_computation.23 | async-start | bytes 1310720 | tf_op jit(solution)/shard_map/all_gather | solution.py:43
  8.7 105.5 %all-gather.15.cloned.1.call-start = ((), (), s32[]{:S(2)}) async-start(), calls=%async_computation.22 | async-start | bytes 2621440 | tf_op jit(solution)/shard_map/all_gather | solution.py:43
  24.0 132.5 %all-gather.19.cloned.1.call-start = ((), (), s32[]{:S(2)}) async-start(), calls=%async_computation.24 | async-start | bytes 2228224 | tf_op jit(solution)/shard_map/all_gather | solution.py:43
  29.6 28.7 %copy-start.49 = (f32[1,2048]{1,0:T(1,128)}, f32[1,2048]{1,0:T(1,128)S(1)}, u32[]{:S(2)}) copy-start(f32[1,2048]{1,0:T(1,128)S(1)} %get-tuple-element.32) | copy-start | bytes 24580
  68.5 12.3 all-to-all-start.1
  71.9 131.5 %all-gather.21.cloned.1.call-start = ((), (), s32[]{:S(2)}) async-start(), calls=%async_computation.25 | async-start | bytes 2621440 | tf_op jit(solution)/shard_map/all_gather | solution.py:43
  81.8 197.1 %reduce-scatter.11.cloned.1.call-start = ((), (), s32[]{:S(2)}) async-start(), calls=%async_computation.26 | async-start | bytes 5242880 | tf_op jit(solution)/shard_map/reduce_scatter | solution.py:47
  119.4 48.5 %copy-start.47 = (bf16[1024,512]{1,0:T(8,128)(2,1)}, bf16[1024,512]{1,0:T(8,128)(2,1)S(1)}, u32[]{:S(2)}) copy-start(bf16[1024,512]{1,0:T(8,128)(2,1)S(1)} %convolution_convert_fusion.10) | copy-start | bytes 3145732
  158.2 23.9 %copy-start.19 = (bf16[4,2,512,256]{3,2,0,1:T(8,128)(2,1)}, bf16[4,2,512,256]{3,2,0,1:T(8,128)(2,1)S(1)}, u32[]{:S(2)}) copy-start(bf16[4,2,512,256]{3,2,0,1:T(8,128)(2,1)S(1)} %copy.68) | copy-start | bytes 6291460
  159.6 16.0 %copy-start.12 = (f32[512,2048]{1,0:T(8,128)}, f32[512,2048]{1,0:T(8,128)S(1)}, u32[]{:S(2)}) copy-start(f32[512,2048]{1,0:T(8,128)S(1)} %get-tuple-element.53) | copy-start | bytes 12582916
  209.8 19.0 %copy-start.45 = (bf16[2,512,512]{2,1,0:T(8,128)(2,1)S(1)}, bf16[2,512,512]{2,1,0:T(8,128)(2,1)}, u32[]{:S(2)}) copy-start(bf16[2,512,512]{2,1,0:T(8,128)(2,1)} %param.14) | copy-start | bytes 3145732
  209.8 136.9 %all-gather.27.cloned.1.call-start = ((), (), s32[]{:S(2)}) async-start(), calls=%async_computation.29 | async-start | bytes 5242880 | tf_op jit(solution)/shard_map/all_gather | solution.py:43
  228.5 173.5 %all-gather.29.cloned.1.call-start = ((), (), s32[]{:S(2)}) async-start(), calls=%async_computation.31 | async-start | bytes 9437184 | tf_op jit(solution)/shard_map/all_gather | solution.py:43
  258.7 225.6 %all-gather.25.cloned.1.call-start = ((), (), s32[]{:S(2)}) async-start(), calls=%async_computation.28 | async-start | bytes 5242880 | tf_op jit(solution)/shard_map/all_gather | solution.py:43
  278.8 260.5 %all-gather.23.cloned.1.call-start = ((), (), s32[]{:S(2)}) async-start(), calls=%async_computation.27 | async-start | bytes 9437184 | tf_op jit(solution)/shard_map/all_gather | solution.py:43
  284.7 361.2 %reduce-scatter.15.cloned.1.call-start = ((), (), s32[]{:S(2)}) async-start(), calls=%async_computation.32 | async-start | bytes 9437184 | tf_op jit(solution)/shard_map/reduce_scatter | solution.py:47
  539.3 24.1 %copy-start.58 = (bf16[1024,2048]{0,1:T(8,128)(2,1)S(1)}, bf16[1024,2048]{0,1:T(8,128)(2,1)}, u32[]{:S(2)}) copy-start(bf16[1024,2048]{0,1:T(8,128)(2,1)} %all-gather.25.cloned.1.call-done) | copy-start | bytes 12582916
  574.5 146.1 %reduce-scatter.13.cloned.1.call-start = ((), (), s32[]{:S(2)}) async-start(), calls=%async_computation.30 | async-start | bytes 9437184 | tf_op jit(solution)/shard_map/reduce_scatter | solution.py:47
  590.1 55.8 %copy-start.38 = (bf16[256,2048]{1,0:T(8,128)(2,1)S(1)}, bf16[256,2048]{1,0:T(8,128)(2,1)}, u32[]{:S(2)}) copy-start(bf16[256,2048]{1,0:T(8,128)(2,1)} %reduce-scatter.11.cloned.1.call-done) | copy-start | bytes 3145732
  590.1 130.4 %copy-start.39 = (bf16[4,32,8,512]{3,2,0,1:T(8,128)(2,1)S(1)}, bf16[4,32,8,512]{3,2,0,1:T(8,128)(2,1)}, u32[]{:S(2)}) copy-start(bf16[4,32,8,512]{3,2,0,1:T(8,128)(2,1)} %copy.95) | copy-start | bytes 3145732
  590.1 170.3 %all-gather.31.cloned.1.call-start = ((), (), s32[]{:S(2)}) async-start(), calls=%async_computation.33 | async-start | bytes 5242880 | tf_op jit(solution)/shard_map/all_gather | solution.py:43
  725.8 184.9 %reduce-scatter.19.cloned.1.call-start = ((), (), s32[]{:S(2)}) async-start(), calls=%async_computation.35 | async-start | bytes 2228224 | tf_op jit(solution)/shard_map/reduce_scatter | solution.py:47
  849.0 140.3 %reduce-scatter.29.cloned.1.call-start = ((), (), s32[]{:S(2)}) async-start(), calls=%async_computation.42 | async-start | bytes 5242880 | tf_op jit(solution)/shard_map/reduce_scatter | solution.py:47
  865.1 203.7 %reduce-scatter.27.cloned.1.call-start = ((), (), s32[]{:S(2)}) async-start(), calls=%async_computation.40 | async-start | bytes 5242880 | tf_op jit(solution)/shard_map/reduce_scatter | solution.py:47
  879.8 235.6 %reduce-scatter.21.cloned.1.call-start = ((), (), s32[]{:S(2)}) async-start(), calls=%async_computation.36 | async-start | bytes 2621440 | tf_op jit(solution)/shard_map/reduce_scatter | solution.py:47
  898.4 262.4 %reduce-scatter.25.cloned.1.call-start = ((), (), s32[]{:S(2)}) async-start(), calls=%async_computation.39 | async-start | bytes 2621440 | tf_op jit(solution)/shard_map/reduce_scatter | solution.py:47
  904.5 283.7 %reduce-scatter.23.cloned.1.call-start = ((), (), s32[]{:S(2)}) async-start(), calls=%async_computation.37 | async-start | bytes 1310720 | tf_op jit(solution)/shard_map/reduce_scatter | solution.py:47
  913.4 309.4 %all-gather.35.cloned.1.call-start = ((), (), s32[]{:S(2)}) async-start(), calls=%async_computation.43 | async-start | bytes 3145728 | tf_op jit(solution)/shard_map/all_gather | solution.py:43
  1008.2 262.8 %reduce-scatter.17.cloned.1.call-start = ((), (), s32[]{:S(2)}) async-start(), calls=%async_computation.34 | async-start | bytes 5242880 | tf_op jit(solution)/shard_map/reduce_scatter | solution.py:47
  1014.3 291.6 %all-gather.33.cloned.1.call-start = ((), (), s32[]{:S(2)}) async-start(), calls=%async_computation.41 | async-start | bytes 3145728 | tf_op jit(solution)/shard_map/all_gather | solution.py:43
  1117.2 45.6 %all-to-all-start.7 = ((bf16[128,4,512]{2,0,1:T(8,128)(2,1)}), bf16[128,4,512]{2,0,1:T(8,128)(2,1)S(1)}, u32[]{:S(2)}, u32[]{:S(2)}) async-start(bf16[128,4,512]{2,0,1:T(8,128)(2,1)} %bitcast.354), calls=%async_computation.13 | async-start | bytes 1048576 | tf_op jit(solution)/shard_map/all_to_all | solution.py:39
  1160.8 66.2 %copy-start.41 = (bf16[256,2048]{1,0:T(8,128)(2,1)S(1)}, bf16[256,2048]{1,0:T(8,128)(2,1)}, u32[]{:S(2)}) copy-start(bf16[256,2048]{1,0:T(8,128)(2,1)} %get-tuple-element.27) | copy-start | bytes 3145732
  1162.8 66.3 %all-to-all-start.8 = ((bf16[128,4,512]{2,0,1:T(8,128)(2,1)}), bf16[128,4,512]{2,0,1:T(8,128)(2,1)S(1)}, u32[]{:S(2)}, u32[]{:S(2)}) async-start(bf16[128,4,512]{2,0,1:T(8,128)(2,1)} %bitcast.353), calls=%async_computation.16 | async-start | bytes 1048576 | tf_op jit(solution)/shard_map/all_to_all | solution.py:39
  1166.3 213.7 %all-reduce.4.cloned.1.call-start = ((), (), s32[]{:S(2)}) async-start(), calls=%async_computation.38 | async-start | bytes 524288 | tf_op jit(solution)/shard_map/psum | solution.py:192
  1227.0 44.0 %copy-start.48 = (bf16[256,256]{1,0:T(8,128)(2,1)S(1)}, bf16[256,256]{1,0:T(8,128)(2,1)}, u32[]{:S(2)}) copy-start(bf16[256,256]{1,0:T(8,128)(2,1)} %reduce-scatter.19.cloned.1.call-done) | copy-start | bytes 393220
  1227.0 44.0 %copy-start.50 = (f32[1,2048]{1,0:T(1,128)S(1)}, f32[1,2048]{1,0:T(1,128)}, u32[]{:S(2)}) copy-start(f32[1,2048]{1,0:T(1,128)} %copy-done.49) | copy-start | bytes 24580
  1229.1 48.1 %all-to-all-start.4 = ((bf16[256,4,512]{2,0,1:T(8,128)(2,1)}), bf16[256,4,512]{2,0,1:T(8,128)(2,1)S(1)}, u32[]{:S(2)}, u32[]{:S(2)}) async-start(bf16[256,4,512]{2,0,1:T(8,128)(2,1)} %bitcast.352), calls=%async_computation.6 | async-start | bytes 2097152 | tf_op jit(solution)/shard_map/all_to_all | solution.py:39
  1232.7 189.7 %all-reduce.6.cloned.1.call-start = ((), (), s32[]{:S(2)}) async-start(), calls=%async_computation.44 | async-start | bytes 2097152 | tf_op jit(solution)/shard_map/psum | solution.py:195
  1232.8 41.3 %copy-start.40 = (f32[256,2048]{1,0:T(8,128)S(1)}, f32[256,2048]{1,0:T(8,128)}, u32[]{:S(2)}) copy-start(f32[256,2048]{1,0:T(8,128)} %get-tuple-element.26) | copy-start | bytes 6291460
  1277.2 189.7 %all-to-all-start.6 = ((bf16[256,4,512]{2,0,1:T(8,128)(2,1)}), bf16[256,4,512]{2,0,1:T(8,128)(2,1)}, u32[]{:S(2)}, u32[]{:S(2)}) async-start(bf16[256,4,512]{2,0,1:T(8,128)(2,1)} %bitcast.351), calls=%async_computation.11 | async-start | bytes 2097152 | tf_op jit(solution)/shard_map/all_to_all | solution.py:39
  1305.9 164.3 %copy-start.1 = (bf16[2048,512]{1,0:T(8,128)(2,1)S(1)}, bf16[2048,512]{1,0:T(8,128)(2,1)}, u32[]{:S(2)}) copy-start(bf16[2048,512]{1,0:T(8,128)(2,1)} %param.23) | copy-start | bytes 6291460
  (41 other events, 235.6 us)
Sparse Core Ops, SparseCore 0:
  9.6 37.4 all-gather.12
  48.7 17.0 all-gather.16
  67.9 46.2 all-gather.14
  116.8 39.6 all-gather.18
  158.4 44.9 all-gather.20
  209.9 53.9 reduce-scatter.10
  266.2 80.5 all-gather.26
  349.4 52.5 all-gather.28
  403.6 80.5 all-gather.24
  486.7 52.5 all-gather.22
  574.6 71.2 reduce-scatter.14
  649.2 71.2 reduce-scatter.12
  725.9 34.4 all-gather.30
  849.1 61.5 reduce-scatter.18
  913.4 75.7 reduce-scatter.28
  991.5 77.2 reduce-scatter.26
  1071.0 44.3 reduce-scatter.20
  1117.6 43.1 reduce-scatter.24
  1163.9 24.2 reduce-scatter.22
  1189.6 33.1 all-gather.34
  1226.1 44.8 reduce-scatter.16
  1273.1 32.7 all-gather.32
  1309.2 70.6 all-reduce.3
  1382.8 39.5 all-reduce.5
